TPU v7x, 32 devices: a whole 2x2x4 slice. The times are simulated.
32 devices in a mesh: band: 4 (over y, x), region: 8 (over z, core).
Axes of the slice: x: 2, y: 2, z: 4, core: 2. Of those that a mesh axis runs over, the one named last changes fastest.
Arguments:
- fields: float32 [8192, 512], P(('band', 'region')), may hold values from -6 to 6
- send_list: int32 [4, 8, 4, 2], replicated, may hold values from -1 to 1, as said below
- departure: int32 [16, 8192], P(None, ('band', 'region')), may hold values from 0 to 1279, as said below
- hweight: float32 [16, 8192], P(None, ('band', 'region')), may hold values from -0.2 to 0.5
- base_level: int32 [128, 8192], P(None, ('band', 'region')), may hold values from 1 to 125
- vweight: float32 [4, 128, 8192], P(None, None, ('band', 'region')), may hold values from -0.25 to 0.75
- vertical_op: float32 [128, 128], replicated, may hold values from -0.4 to 2, as said below
Outputs:
- level_shards: float32 [512, 8192], P('region', 'band')
Inputs may be any that keep to these rules, and one draw needn't show every extreme that they name: send_list[b, r, d] names distinct block numbers of device (b, r), each block being 128 consecutive points of it; a list holds 1 to 2 numbers followed by -1 in the remaining entries, and in every draw some region's lists are all full. departure[c, p] indexes the extended rows of point p's device: below 256 the device's own point, else 256 + d * 2 * 128 + s for row s of part d; only rows delivered by an existing neighbour from a list entry that is not -1 are named. vertical_op[k, l] is zero where k and l differ by more than 2.
All inputs are finite; a program needn't handle non-finite values.
Results may differ from a plain program's by a relative error of at most 0.0003.
Values sent between devices are 32-bit elements; how exact they have to be, the bound alone decides.
No kernel may reach another device: no remote copies, remote signals or barrier semaphores. Data moves between devices by JAX's collectives and lax.ppermute only.
A program may use at most 64 MiB of HBM per device.

v0:
```python
import jax
import jax.numpy as jnp
from jax import lax
from jax.sharding import PartitionSpec as P

BLK = 128
exact_mode = lax.Precision.HIGHEST


def from_behind(block, axis, distance):
    devices = range(lax.axis_size(axis))
    route = [(i - distance, i) for i in devices if i - distance in devices]
    return lax.ppermute(block, axis, route)


def from_behind_2(block, axis, distance):
    devices = range(lax.axis_size(axis))
    route = [((i - distance) % len(devices), i) for i in devices]
    return lax.ppermute(block, axis, route)


def padded_2(x, sides, width):
    for axis, dim in sides:
        size, length = (lax.axis_size(axis), x.shape[dim])
        up = [(i, (i + 1) % size) for i in range(size - 1)]
        down = [(j, i) for i, j in up]
        last = lax.slice_in_dim(x, length - width, length, axis=dim)
        initial = lax.slice_in_dim(x, 0, width, axis=dim)
        before = lax.ppermute(last, axis, up)
        after = lax.ppermute(initial, axis, down)
        x = jnp.concatenate([before, x, after], axis=dim)
    return x


def pack_blocks(block_table, block_list):
    safe_list = jnp.maximum(block_list, 0)
    picked = jnp.take(block_table, safe_list, axis=0)
    keeping = (block_list >= 0)[:, None, None]
    picked = jnp.where(keeping, picked, jnp.zeros((), picked.dtype))
    return picked.reshape(-1, picked.shape[-1])


def column_update(extended, depart_block, hweight_block, base_block, vweight_block, vertical_op):
    stencil_len, point_count = depart_block.shape
    width_all = extended.shape[1]
    levels = vertical_op.shape[0]
    fields_count = width_all // levels
    picked = jnp.take(extended, depart_block.reshape(-1), axis=0).reshape(
        stencil_len, point_count, width_all
    )
    horizontal = jnp.sum(hweight_block[:, :, None] * picked, axis=0)
    stacked = jnp.transpose(horizontal).reshape(fields_count, levels, point_count)
    source_ids = jnp.arange(levels, dtype=jnp.int32)[None, :, None]
    level_weights = jnp.zeros((levels, levels, point_count), jnp.float32)
    for offset in range(4):
        target = (base_block + (offset - 1))[:, None, :]
        level_weights = level_weights + jnp.where(
            target == source_ids, vweight_block[offset][:, None, :], jnp.zeros((), jnp.float32)
        )
    interpolated = jnp.einsum("klp,flp->fkp", level_weights, stacked, precision=exact_mode)
    return interpolated.reshape(width_all, point_count)


def body(fields, send_list, departure, hweight, base_level, vweight, vertical_op):
    point_total, width_all = fields.shape
    levels = vertical_op.shape[0]
    block_table = fields.reshape(point_total // BLK, BLK, width_all)
    band_id = lax.axis_index("band")
    region_id = lax.axis_index("region")
    region_count = lax.axis_size("region")
    own_lists = send_list[band_id, region_id]
    from_north = from_behind(pack_blocks(block_table, own_lists[0]), "band", 1)
    from_south = from_behind(pack_blocks(block_table, own_lists[1]), "band", -1)
    from_west = from_behind_2(pack_blocks(block_table, own_lists[2]), "region", 1)
    from_east = from_behind_2(pack_blocks(block_table, own_lists[3]), "region", -1)
    extended = jnp.concatenate([fields, from_north, from_south, from_west, from_east], axis=0)
    step_points = min(128, point_total)

    def one_step(step_id, result):
        first_col = step_id * step_points
        updated = column_update(
            extended,
            lax.dynamic_slice_in_dim(departure, first_col, step_points, 1),
            lax.dynamic_slice_in_dim(hweight, first_col, step_points, 1),
            lax.dynamic_slice_in_dim(base_level, first_col, step_points, 1),
            lax.dynamic_slice_in_dim(vweight, first_col, step_points, 2),
            vertical_op,
        )
        return lax.dynamic_update_slice_in_dim(result, updated, first_col, 1)

    result = lax.fori_loop(
        0, point_total // step_points, one_step, jnp.zeros((width_all, point_total), jnp.float32)
    )
    shard_rows = lax.all_to_all(result, "region", split_axis=0, concat_axis=1, tiled=True)
    row_count = width_all // region_count
    padded = padded_2(shard_rows, (("region", 0),), 2)
    global_rows = region_id * row_count + jnp.arange(row_count, dtype=jnp.int32)
    level_ids = global_rows % levels
    operated = jnp.zeros(shard_rows.shape, jnp.float32)
    for offset in range(-2, 3):
        target = level_ids + offset
        valid = (target >= 0) & (target < levels)
        coeff = vertical_op[level_ids, jnp.clip(target, 0, levels - 1)]
        coeff = jnp.where(valid, coeff, jnp.zeros((), jnp.float32))
        operated = operated + coeff[:, None] * padded[2 + offset : 2 + offset + row_count, :]
    return operated


def solution(mesh):
    placed = (
        P(("band", "region"), None),
        P(),
        P(None, ("band", "region")),
        P(None, ("band", "region")),
        P(None, ("band", "region")),
        P(None, None, ("band", "region")),
        P(),
    )
    return jax.shard_map(
        body, mesh=mesh, in_specs=placed, out_specs=P("region", "band"), check_vma=False
    )
```

profile of v0, /device:TPU:1, one launch (start us, length us, event | category | flops | bytes accessed | tf_op | source)
XLA Modules:
  0.0 178.1 jit_solution(16740423676924799088)
XLA Ops:
  0.0 1.0 maximum_reduce_fusion
  1.0 1.0 compare_reduce_fusion
  2.0 1.6 gather_fusion.6
  3.6 0.9 select_select_fusion.3
  4.6 4.7 %collective-permute-start = (f32[256,512]{1,0:T(8,128)}, f32[256,512]{1,0:T(8,128)}, u32[]{:S(2)}, u32[]{:S(2)}) collective-permute-start(f32[256,512]{1,0:T(8,128)} %bitcast.11), channel_id=1, source_target_pairs={{0,8},{8,16},{16,24},{1,9},{9,17},{17,25},{2,10},{10,18},{18,26},{... | collective-permute-start | bytes 1572872 | tf_op jit(solution)/shard_map/ppermute | solution.py:13
  9.3 1.6 gather_fusion.7
  10.9 0.9 select_select_fusion.2
  11.9 1.3 collective-permute-start.1
  13.2 0.6 gather_fusion.8
  13.8 0.9 select_select_fusion.1
  14.8 2.1 %collective-permute-start.2 = (f32[256,512]{1,0:T(8,128)}, f32[256,512]{1,0:T(8,128)}, u32[]{:S(2)}, u32[]{:S(2)}) collective-permute-start(f32[256,512]{1,0:T(8,128)} %bitcast.13), channel_id=1, source_target_pairs={{7,0},{0,1},{1,2},{2,3},{3,4},{4,5},{5,6},{6,7},{15,8},{8,9},{9,10... | collective-permute-start | bytes 1572872 | tf_op jit(solution)/shard_map/ppermute | solution.py:19
  16.9 0.6 gather_fusion.9
  17.5 0.9 select_select_fusion
  18.4 0.0 collective-permute-start.3
  18.5 0.9 collective-permute-done
  19.4 1.1 constant_dynamic-update-slice_fusion.4
  20.5 12.1 %collective-permute-done.1 = f32[256,512]{1,0:T(8,128)} collective-permute-done((f32[256,512]{1,0:T(8,128)}, f32[256,512]{1,0:T(8,128)}, u32[]{:S(2)}, u32[]{:S(2)}) %collective-permute-start.1) | collective-permute-done | bytes 524320 | tf_op jit(solution)/shard_map/ppermute | solution.py:13
  32.6 1.1 constant_dynamic-update-slice_fusion.3
  33.7 0.0 collective-permute-done.2
  33.7 1.1 constant_dynamic-update-slice_fusion.2
  34.8 1.1 constant_dynamic-update-slice_fusion.1
  35.9 0.8 broadcast_in_dim.186.clone
  36.7 112.9 %while.13 = (s32[]{:T(128)}, f32[512,256]{1,0:T(8,128)}, f32[16,256]{1,0:T(8,128)}, s32[16,256]{1,0:T(8,128)}, f32[1280,512]{1,0:T(8,128)S(1)}, /*index=5*/s32[1...) while((s32[]{:T(128)}, f32[512,256]{1,0:T(8,128)}, ...), condition=%wide.region_2.4_spmd, body=%wide.region_0.3_spmd.sunk | while | flops 126881800 | bytes 17125624 | solution.py:91
  36.7 0.7 compare_and_fusion.6
  37.4 8.9 %gather_fusion = f32[2048,512]{1,0:T(8,128)} fusion(f32[1280,512]{1,0:T(8,128)S(1)} %get-tuple-element.290, s32[2048]{0:T(1024)S(1)} %broadcast_clamp_fusion.2), kind=kCustom, calls=%fused_computation.1.clone.1 | custom fusion | bytes 8396800 | tf_op jit(solution)/shard_map/while/body/eval_jaxpr/jit(_take)/gather | solution.py:48
  46.3 0.7 constant_dynamic-slice_fusion.15
  47.0 2.6 %multiply_reduce_fusion.2 = f32[128,512]{1,0:T(8,128)S(1)} fusion(f32[16,128,512]{2,1,0:T(8,128)} %bitcast.59, f32[16,128]{1,0:T(8,128)S(1)} %constant_dynamic-slice_fusion.15, pred[16,128]{1,0:T(8,128)(4,1)S(1)} %get-tuple-element.250), kind=kLoop, calls=%fused_computation.31.clone.1 | loop fusion | flops 3080192 | bytes 4466688 | tf_op jit(solution)/shard_map/while/body/eval_jaxpr/reduce_sum | solution.py:51
  49.6 0.1 reshape.413
  49.7 1.0 constant_dynamic-slice_fusion.16
  50.7 0.1 copy.34
  50.8 0.1 copy.36
  50.9 0.1 copy.37
  51.0 0.1 copy.38
  51.1 0.9 constant_dynamic-slice_fusion.17
  51.9 0.1 copy.35
  52.1 40.2 %fusion.62 = f32[4,128,128]{1,0,2:T(4,128)S(1)} fusion(f32[4,128,128]{1,0,2:T(4,128)S(1)} %reshape.413, f32[128,128]{0,1:T(8,128)S(1)} %bitcast.71, s32[128,128]{0,1:T(8,128)S(1)} %get-tuple-element.252, f32[128,128]{0,1:T(8,128)S(1)} %bitcast.72, s32[128,128]{0,1:T(8,128)S(1)} %get-tuple-element.254, f32[128,128]{0,1:T(8,128)S(1)} %bitcast.73, ...), kind=kOutput, calls=%fused_computation.32.clone.2 | convolution fusion | flops 123731968 | bytes 1048576 | tf_op jit(solution)/shard_map/while/body/eval_jaxpr/klp,flp->fkp/dot_general | solution.py:60
  92.2 0.1 copy.39
  92.4 0.7 constant_dynamic-update-slice_fusion.9
  93.1 0.7 compare_and_fusion.6
  93.9 8.9 %gather_fusion = f32[2048,512]{1,0:T(8,128)} fusion(f32[1280,512]{1,0:T(8,128)S(1)} %get-tuple-element.290, s32[2048]{0:T(1024)S(1)} %broadcast_clamp_fusion.2), kind=kCustom, calls=%fused_computation.1.clone.1 | custom fusion | bytes 8396800 | tf_op jit(solution)/shard_map/while/body/eval_jaxpr/jit(_take)/gather | solution.py:48
  102.8 0.7 constant_dynamic-slice_fusion.15
  103.5 2.6 %multiply_reduce_fusion.2 = f32[128,512]{1,0:T(8,128)S(1)} fusion(f32[16,128,512]{2,1,0:T(8,128)} %bitcast.59, f32[16,128]{1,0:T(8,128)S(1)} %constant_dynamic-slice_fusion.15, pred[16,128]{1,0:T(8,128)(4,1)S(1)} %get-tuple-element.250), kind=kLoop, calls=%fused_computation.31.clone.1 | loop fusion | flops 3080192 | bytes 4466688 | tf_op jit(solution)/shard_map/while/body/eval_jaxpr/reduce_sum | solution.py:51
  106.1 0.1 reshape.413
  106.2 1.0 constant_dynamic-slice_fusion.16
  107.1 0.1 copy.34
  107.2 0.1 copy.36
  107.3 0.1 copy.37
  107.4 0.1 copy.38
  107.5 0.9 constant_dynamic-slice_fusion.17
  108.4 0.1 copy.35
  108.5 40.2 %fusion.62 = f32[4,128,128]{1,0,2:T(4,128)S(1)} fusion(f32[4,128,128]{1,0,2:T(4,128)S(1)} %reshape.413, f32[128,128]{0,1:T(8,128)S(1)} %bitcast.71, s32[128,128]{0,1:T(8,128)S(1)} %get-tuple-element.252, f32[128,128]{0,1:T(8,128)S(1)} %bitcast.72, s32[128,128]{0,1:T(8,128)S(1)} %get-tuple-element.254, f32[128,128]{0,1:T(8,128)S(1)} %bitcast.73, ...), kind=kOutput, calls=%fused_computation.32.clone.2 | convolution fusion | flops 123731968 | bytes 1048576 | tf_op jit(solution)/shard_map/while/body/eval_jaxpr/klp,flp->fkp/dot_general | solution.py:60
  148.7 0.1 copy.39
  148.9 0.7 constant_dynamic-update-slice_fusion.9
  149.6 6.4 %all-to-all-start = ((f32[8,64,256]{2,1,0:T(8,128)}), f32[8,64,256]{2,1,0:T(8,128)S(1)}, u32[]{:S(2)}, u32[]{:S(2)}) async-start(f32[8,64,256]{2,1,0:T(8,128)} %bitcast.70), calls=%async_computation | async-start | bytes 1048576 | tf_op jit(solution)/shard_map/all_to_all | solution.py:94
  156.0 0.8 gather_fusion.4
  156.8 0.8 gather_fusion.5
  157.6 0.8 gather_fusion.2
  158.4 0.8 gather_fusion.3
  159.2 0.8 gather_fusion.1
  160.1 10.3 %all-to-all-done = f32[8,64,256]{2,1,0:T(8,128)S(1)} async-done(((f32[8,64,256]{2,1,0:T(8,128)}), f32[8,64,256]{2,1,0:T(8,128)S(1)}, u32[]{:S(2)}, u32[]{:S(2)}) %all-to-all-start) | async-done | bytes 524320 | tf_op jit(solution)/shard_map/all_to_all | solution.py:94
  170.4 2.9 %collective-permute-start.5 = (f32[2,2048]{1,0:T(2,128)S(1)}, f32[2,2048]{1,0:T(2,128)S(1)}, u32[]{:S(2)}, u32[]{:S(2)}) collective-permute-start(f32[2,2048]{1,0:T(2,128)S(1)} %bitcast.78), channel_id=1, source_target_pairs={{1,0},{2,1},{3,2},{4,3},{5,4},{6,5},{7,6},{9,8},{10,9},{11,10},{12... | collective-permute-start | bytes 49160 | tf_op jit(solution)/shard_map/ppermute | solution.py:30
  173.3 2.7 %collective-permute-start.4 = (f32[2,2048]{1,0:T(2,128)S(1)}, f32[2,2048]{1,0:T(2,128)S(1)}, u32[]{:S(2)}, u32[]{:S(2)}) collective-permute-start(f32[2,2048]{1,0:T(2,128)S(1)} %bitcast.77), channel_id=1, source_target_pairs={{0,1},{1,2},{2,3},{3,4},{4,5},{5,6},{6,7},{8,9},{9,10},{10,11},{11... | collective-permute-start | bytes 49160 | tf_op jit(solution)/shard_map/ppermute | solution.py:29
  176.1 0.8 collective-permute-done.4
  176.9 1.2 fusion.26
  (33 shorter events, 0.4 us)
Async XLA Ops:
  0.0 156.0 %copy-start = (f32[128,128]{1,0:T(8,128)S(1)}, f32[128,128]{1,0:T(8,128)}, u32[]{:S(2)}) copy-start(f32[128,128]{1,0:T(8,128)} %param.17) | copy-start | bytes 196612
  0.0 13.2 %copy-start.1 = (f32[256,512]{1,0:T(8,128)S(1)}, f32[256,512]{1,0:T(8,128)}, u32[]{:S(2)}) copy-start(f32[256,512]{1,0:T(8,128)} %param.11) | copy-start | bytes 1572868
  4.6 14.8 %collective-permute-start = (f32[256,512]{1,0:T(8,128)}, f32[256,512]{1,0:T(8,128)}, u32[]{:S(2)}, u32[]{:S(2)}) collective-permute-start(f32[256,512]{1,0:T(8,128)} %bitcast.11), channel_id=1, source_target_pairs={{0,8},{8,16},{16,24},{1,9},{9,17},{17,25},{2,10},{10,18},{18,26},{... | collective-permute-start | bytes 1572872 | tf_op jit(solution)/shard_map/ppermute | solution.py:13
  11.9 20.7 %collective-permute-start.1 = (f32[256,512]{1,0:T(8,128)}, f32[256,512]{1,0:T(8,128)}, u32[]{:S(2)}, u32[]{:S(2)}) collective-permute-start(f32[256,512]{1,0:T(8,128)} %bitcast.12), channel_id=1, source_target_pairs={{8,0},{16,8},{24,16},{9,1},{17,9},{25,17},{10,2},{18,10},{26,18},{... | collective-permute-start | bytes 1572872 | tf_op jit(solution)/shard_map/ppermute | solution.py:13
  14.8 18.9 %collective-permute-start.2 = (f32[256,512]{1,0:T(8,128)}, f32[256,512]{1,0:T(8,128)}, u32[]{:S(2)}, u32[]{:S(2)}) collective-permute-start(f32[256,512]{1,0:T(8,128)} %bitcast.13), channel_id=1, source_target_pairs={{7,0},{0,1},{1,2},{2,3},{3,4},{4,5},{5,6},{6,7},{15,8},{8,9},{9,10... | collective-permute-start | bytes 1572872 | tf_op jit(solution)/shard_map/ppermute | solution.py:19
  18.4 16.3 %collective-permute-start.3 = (f32[256,512]{1,0:T(8,128)}, f32[256,512]{1,0:T(8,128)}, u32[]{:S(2)}, u32[]{:S(2)}) collective-permute-start(f32[256,512]{1,0:T(8,128)} %bitcast.14), channel_id=1, source_target_pairs={{1,0},{2,1},{3,2},{4,3},{5,4},{6,5},{7,6},{0,7},{9,8},{10,9},{11,1... | collective-permute-start | bytes 1572872 | tf_op jit(solution)/shard_map/ppermute | solution.py:19
  149.6 20.8 %all-to-all-start = ((f32[8,64,256]{2,1,0:T(8,128)}), f32[8,64,256]{2,1,0:T(8,128)S(1)}, u32[]{:S(2)}, u32[]{:S(2)}) async-start(f32[8,64,256]{2,1,0:T(8,128)} %bitcast.70), calls=%async_computation | async-start | bytes 1048576 | tf_op jit(solution)/shard_map/all_to_all | solution.py:94
  170.4 5.6 %collective-permute-start.5 = (f32[2,2048]{1,0:T(2,128)S(1)}, f32[2,2048]{1,0:T(2,128)S(1)}, u32[]{:S(2)}, u32[]{:S(2)}) collective-permute-start(f32[2,2048]{1,0:T(2,128)S(1)} %bitcast.78), channel_id=1, source_target_pairs={{1,0},{2,1},{3,2},{4,3},{5,4},{6,5},{7,6},{9,8},{10,9},{11,10},{12... | collective-permute-start | bytes 49160 | tf_op jit(solution)/shard_map/ppermute | solution.py:30
  173.3 3.5 %collective-permute-start.4 = (f32[2,2048]{1,0:T(2,128)S(1)}, f32[2,2048]{1,0:T(2,128)S(1)}, u32[]{:S(2)}, u32[]{:S(2)}) collective-permute-start(f32[2,2048]{1,0:T(2,128)S(1)} %bitcast.77), channel_id=1, source_target_pairs={{0,1},{1,2},{2,3},{3,4},{4,5},{5,6},{6,7},{8,9},{9,10},{10,11},{11... | collective-permute-start | bytes 49160 | tf_op jit(solution)/shard_map/ppermute | solution.py:29
where the time goes:
time: 179 us; the launch traced here: 178 us
  matrix products  80.4 us (45%)
  local copies, waits for them, and re-layouts  39.3 us (22%)
  waiting for transfers between devices  24.1 us (13%)
  starting transfers between devices  20.1 us (11%)
  other arithmetic  13.8 us (8%)
    dot_general x2, matrix products, column_update(): jnp.einsum('klp,flp->fkp', level_weights, stacked, precision=exact_mode)  80.4 us
    gather x2, local copies, waits for them, and re-layouts, column_update(): jnp.take(extended, depart_block.reshape(-1), axis=0)  17.8 us
    ppermute x2, waiting for transfers between devices, from_behind(): return lax.ppermute(block, axis, route)  13 us
    all_to_all x1, waiting for transfers between devices, body(): lax.all_to_all(result, 'region', split_axis=0, concat_axis=1, tiled=True)  10.3 us
    all_to_all x1, starting transfers between devices, body(): lax.all_to_all(result, 'region', split_axis=0, concat_axis=1, tiled=True)  6.4 us
    ppermute x2, starting transfers between devices, from_behind(): return lax.ppermute(block, axis, route)  6 us
    reduce_sum x2, other arithmetic, column_update(): horizontal = jnp.sum(hweight_block[:, :, None] * picked, axis=0)  5.2 us
    gather x4, local copies, waits for them, and re-layouts, pack_blocks(): picked = jnp.take(block_table, safe_list, axis=0)  4.4 us
  transfers between devices with their start and end apart: 7, of which 4 were waited for; matrix products, arithmetic and copies ran while one was open for 7% of the time, Pallas kernels for 0%

commit v1 on v0

--- a/solution.py
+++ b/solution.py
@@ -91,7 +91,12 @@
     result = lax.fori_loop(
         0, point_total // step_points, one_step, jnp.zeros((width_all, point_total), jnp.float32)
     )
-    shard_rows = lax.all_to_all(result, "region", split_axis=0, concat_axis=1, tiled=True)
+    shard_rows = jnp.concatenate(
+        lax.all_to_all(
+            jnp.stack(jnp.split(result, lax.axis_size("region"), axis=0)), "region", 0, 0
+        ),
+        axis=1,
+    )
     row_count = width_all // region_count
     padded = padded_2(shard_rows, (("region", 0),), 2)
     global_rows = region_id * row_count + jnp.arange(row_count, dtype=jnp.int32)

time: 179 us -> 191 us (1.067)
  local copies, waits for them, and re-layouts: 39.3 us -> 51 us
    unnamed x9 -> x16, local copies, waits for them, and re-layouts: 3.31 us -> 13.5 us
where the time goes in v1:
time: 191 us; the launch traced here: 190 us
  matrix products  80.4 us (42%)
  local copies, waits for them, and re-layouts  51 us (27%)
  waiting for transfers between devices  24.1 us (13%)
  starting transfers between devices  20.1 us (11%)
  other arithmetic  13.8 us (7%)
    dot_general x2, matrix products, column_update(): jnp.einsum('klp,flp->fkp', level_weights, stacked, precision=exact_mode)  80.4 us
    gather x2, local copies, waits for them, and re-layouts, column_update(): jnp.take(extended, depart_block.reshape(-1), axis=0)  17.8 us
    unnamed x16, local copies, waits for them, and re-layouts  13.5 us
    ppermute x2, waiting for transfers between devices, from_behind(): return lax.ppermute(block, axis, route)  13 us
    all_to_all x1, waiting for transfers between devices, body(): lax.all_to_all(jnp.stack(jnp.split(result, lax.axis_size('region'), axis=...  10.3 us
    all_to_all x1, starting transfers between devices, body(): lax.all_to_all(jnp.stack(jnp.split(result, lax.axis_size('region'), axis=...  6.4 us
    ppermute x2, starting transfers between devices, from_behind(): return lax.ppermute(block, axis, route)  6 us
    reduce_sum x2, other arithmetic, column_update(): horizontal = jnp.sum(hweight_block[:, :, None] * picked, axis=0)  5.2 us
  transfers between devices with their start and end apart: 7, of which 4 were waited for; matrix products, arithmetic and copies ran while one was open for 7% of the time, Pallas kernels for 0%

profile of v1, /device:TPU:1, one launch (start us, length us, event | category | flops | bytes accessed | tf_op | source)
XLA Modules:
  0.0 189.8 jit_solution(16045560498128963384)
XLA Ops:
  0.0 1.0 maximum_reduce_fusion
  1.0 1.0 compare_reduce_fusion
  2.0 1.6 gather_fusion.6
  3.6 0.9 select_select_fusion.3
  4.6 4.7 %collective-permute-start = (f32[256,512]{1,0:T(8,128)}, f32[256,512]{1,0:T(8,128)}, u32[]{:S(2)}, u32[]{:S(2)}) collective-permute-start(f32[256,512]{1,0:T(8,128)} %bitcast.11), channel_id=1, source_target_pairs={{0,8},{8,16},{16,24},{1,9},{9,17},{17,25},{2,10},{10,18},{18,26},{... | collective-permute-start | bytes 1572872 | tf_op jit(solution)/shard_map/ppermute | solution.py:13
  9.3 1.6 gather_fusion.7
  10.9 0.9 select_select_fusion.2
  11.9 1.3 collective-permute-start.1
  13.2 0.6 gather_fusion.8
  13.8 0.9 select_select_fusion.1
  14.8 2.1 %collective-permute-start.2 = (f32[256,512]{1,0:T(8,128)}, f32[256,512]{1,0:T(8,128)}, u32[]{:S(2)}, u32[]{:S(2)}) collective-permute-start(f32[256,512]{1,0:T(8,128)} %bitcast.13), channel_id=1, source_target_pairs={{7,0},{0,1},{1,2},{2,3},{3,4},{4,5},{5,6},{6,7},{15,8},{8,9},{9,10... | collective-permute-start | bytes 1572872 | tf_op jit(solution)/shard_map/ppermute | solution.py:19
  16.9 0.6 gather_fusion.9
  17.5 0.9 select_select_fusion
  18.5 0.9 collective-permute-done
  19.4 1.1 constant_dynamic-update-slice_fusion.4
  20.5 12.1 %collective-permute-done.1 = f32[256,512]{1,0:T(8,128)} collective-permute-done((f32[256,512]{1,0:T(8,128)}, f32[256,512]{1,0:T(8,128)}, u32[]{:S(2)}, u32[]{:S(2)}) %collective-permute-start.1) | collective-permute-done | bytes 524320 | tf_op jit(solution)/shard_map/ppermute | solution.py:13
  32.6 1.1 constant_dynamic-update-slice_fusion.3
  33.7 1.1 constant_dynamic-update-slice_fusion.2
  34.8 1.1 constant_dynamic-update-slice_fusion.1
  35.9 0.8 broadcast_in_dim.186.clone
  36.7 112.9 %while.13 = (s32[]{:T(128)}, f32[512,256]{1,0:T(8,128)}, f32[16,256]{1,0:T(8,128)}, s32[16,256]{1,0:T(8,128)}, f32[1280,512]{1,0:T(8,128)S(1)}, /*index=5*/s32[1...) while((s32[]{:T(128)}, f32[512,256]{1,0:T(8,128)}, ...), condition=%wide.region_2.4_spmd, body=%wide.region_0.3_spmd.sunk | while | flops 126881800 | bytes 17125624 | solution.py:91
  36.7 0.7 compare_and_fusion.6
  37.4 8.9 %gather_fusion = f32[2048,512]{1,0:T(8,128)} fusion(f32[1280,512]{1,0:T(8,128)S(1)} %get-tuple-element.297, s32[2048]{0:T(1024)S(1)} %broadcast_clamp_fusion.2), kind=kCustom, calls=%fused_computation.1.clone.1 | custom fusion | bytes 8396800 | tf_op jit(solution)/shard_map/while/body/eval_jaxpr/jit(_take)/gather | solution.py:48
  46.3 0.7 constant_dynamic-slice_fusion.15
  47.0 2.6 %multiply_reduce_fusion.2 = f32[128,512]{1,0:T(8,128)S(1)} fusion(f32[16,128,512]{2,1,0:T(8,128)} %bitcast.74, f32[16,128]{1,0:T(8,128)S(1)} %constant_dynamic-slice_fusion.15, pred[16,128]{1,0:T(8,128)(4,1)S(1)} %get-tuple-element.257), kind=kLoop, calls=%fused_computation.31.clone.1 | loop fusion | flops 3080192 | bytes 4466688 | tf_op jit(solution)/shard_map/while/body/eval_jaxpr/reduce_sum | solution.py:51
  49.7 1.0 constant_dynamic-slice_fusion.16
  50.8 0.1 copy.57
  50.9 0.1 copy.58
  51.0 0.1 copy.59
  51.1 0.9 constant_dynamic-slice_fusion.17
  52.1 40.2 %fusion.62 = f32[4,128,128]{1,0,2:T(4,128)S(1)} fusion(f32[4,128,128]{1,0,2:T(4,128)S(1)} %reshape.418, f32[128,128]{0,1:T(8,128)S(1)} %bitcast.85, s32[128,128]{0,1:T(8,128)S(1)} %get-tuple-element.259, f32[128,128]{0,1:T(8,128)S(1)} %bitcast.86, s32[128,128]{0,1:T(8,128)S(1)} %get-tuple-element.261, f32[128,128]{0,1:T(8,128)S(1)} %bitcast.87, ...), kind=kOutput, calls=%fused_computation.32.clone.2 | convolution fusion | flops 123731968 | bytes 1048576 | tf_op jit(solution)/shard_map/while/body/eval_jaxpr/klp,flp->fkp/dot_general | solution.py:60
  92.2 0.1 copy.60
  92.4 0.7 constant_dynamic-update-slice_fusion.9
  93.1 0.7 compare_and_fusion.6
  93.9 8.9 %gather_fusion = f32[2048,512]{1,0:T(8,128)} fusion(f32[1280,512]{1,0:T(8,128)S(1)} %get-tuple-element.297, s32[2048]{0:T(1024)S(1)} %broadcast_clamp_fusion.2), kind=kCustom, calls=%fused_computation.1.clone.1 | custom fusion | bytes 8396800 | tf_op jit(solution)/shard_map/while/body/eval_jaxpr/jit(_take)/gather | solution.py:48
  102.8 0.7 constant_dynamic-slice_fusion.15
  103.5 2.6 %multiply_reduce_fusion.2 = f32[128,512]{1,0:T(8,128)S(1)} fusion(f32[16,128,512]{2,1,0:T(8,128)} %bitcast.74, f32[16,128]{1,0:T(8,128)S(1)} %constant_dynamic-slice_fusion.15, pred[16,128]{1,0:T(8,128)(4,1)S(1)} %get-tuple-element.257), kind=kLoop, calls=%fused_computation.31.clone.1 | loop fusion | flops 3080192 | bytes 4466688 | tf_op jit(solution)/shard_map/while/body/eval_jaxpr/reduce_sum | solution.py:51
  106.2 1.0 constant_dynamic-slice_fusion.16
  107.2 0.1 copy.57
  107.3 0.1 copy.58
  107.4 0.1 copy.59
  107.5 0.9 constant_dynamic-slice_fusion.17
  108.5 40.2 %fusion.62 = f32[4,128,128]{1,0,2:T(4,128)S(1)} fusion(f32[4,128,128]{1,0,2:T(4,128)S(1)} %reshape.418, f32[128,128]{0,1:T(8,128)S(1)} %bitcast.85, s32[128,128]{0,1:T(8,128)S(1)} %get-tuple-element.259, f32[128,128]{0,1:T(8,128)S(1)} %bitcast.86, s32[128,128]{0,1:T(8,128)S(1)} %get-tuple-element.261, f32[128,128]{0,1:T(8,128)S(1)} %bitcast.87, ...), kind=kOutput, calls=%fused_computation.32.clone.2 | convolution fusion | flops 123731968 | bytes 1048576 | tf_op jit(solution)/shard_map/while/body/eval_jaxpr/klp,flp->fkp/dot_general | solution.py:60
  148.7 0.1 copy.60
  148.9 0.7 constant_dynamic-update-slice_fusion.9
  149.6 1.5 bitcast_dynamic-update-slice_fusion.7
  151.0 1.5 bitcast_dynamic-update-slice_fusion.6
  152.5 1.5 bitcast_dynamic-update-slice_fusion.5
  154.0 1.5 bitcast_dynamic-update-slice_fusion.4
  155.4 1.5 bitcast_dynamic-update-slice_fusion.3
  156.9 1.5 bitcast_dynamic-update-slice_fusion.2
  158.4 1.5 bitcast_dynamic-update-slice_fusion.1
  159.8 1.5 bitcast_dynamic-update-slice_fusion
  161.3 6.4 %all-to-all-start = ((f32[8,64,256]{2,1,0:T(8,128)}), f32[8,64,256]{2,1,0:T(8,128)S(1)}, u32[]{:S(2)}, u32[]{:S(2)}) async-start(f32[8,64,256]{2,1,0:T(8,128)} %bitcast_dynamic-update-slice_fusion), calls=%async_computation | async-start | bytes 1048576 | tf_op jit(solution)/shard_map/all_to_all | solution.py:95
  167.7 0.8 gather_fusion.4
  168.5 0.8 gather_fusion.5
  169.3 0.8 gather_fusion.2
  170.1 0.8 gather_fusion.3
  170.9 0.8 gather_fusion.1
  171.8 10.3 %all-to-all-done = f32[8,64,256]{2,1,0:T(8,128)S(1)} async-done(((f32[8,64,256]{2,1,0:T(8,128)}), f32[8,64,256]{2,1,0:T(8,128)S(1)}, u32[]{:S(2)}, u32[]{:S(2)}) %all-to-all-start) | async-done | bytes 524320 | tf_op jit(solution)/shard_map/all_to_all | solution.py:95
  182.1 2.9 %collective-permute-start.5 = (f32[2,2048]{1,0:T(2,128)S(1)}, f32[2,2048]{1,0:T(2,128)S(1)}, u32[]{:S(2)}, u32[]{:S(2)}) collective-permute-start(f32[2,2048]{1,0:T(2,128)S(1)} %bitcast.92), channel_id=1, source_target_pairs={{1,0},{2,1},{3,2},{4,3},{5,4},{6,5},{7,6},{9,8},{10,9},{11,10},{12... | collective-permute-start | bytes 49160 | tf_op jit(solution)/shard_map/ppermute | solution.py:30
  185.0 2.7 %collective-permute-start.4 = (f32[2,2048]{1,0:T(2,128)S(1)}, f32[2,2048]{1,0:T(2,128)S(1)}, u32[]{:S(2)}, u32[]{:S(2)}) collective-permute-start(f32[2,2048]{1,0:T(2,128)S(1)} %bitcast.91), channel_id=1, source_target_pairs={{0,1},{1,2},{2,3},{3,4},{4,5},{5,6},{6,7},{8,9},{9,10},{10,11},{11... | collective-permute-start | bytes 49160 | tf_op jit(solution)/shard_map/ppermute | solution.py:29
  187.8 0.8 collective-permute-done.4
  188.6 1.2 fusion.26
  (41 shorter events, 0.9 us)
Async XLA Ops:
  0.0 167.7 %copy-start = (f32[128,128]{1,0:T(8,128)S(1)}, f32[128,128]{1,0:T(8,128)}, u32[]{:S(2)}) copy-start(f32[128,128]{1,0:T(8,128)} %param.17) | copy-start | bytes 196612
  0.0 13.2 %copy-start.1 = (f32[256,512]{1,0:T(8,128)S(1)}, f32[256,512]{1,0:T(8,128)}, u32[]{:S(2)}) copy-start(f32[256,512]{1,0:T(8,128)} %param.11) | copy-start | bytes 1572868
  4.6 14.8 %collective-permute-start = (f32[256,512]{1,0:T(8,128)}, f32[256,512]{1,0:T(8,128)}, u32[]{:S(2)}, u32[]{:S(2)}) collective-permute-start(f32[256,512]{1,0:T(8,128)} %bitcast.11), channel_id=1, source_target_pairs={{0,8},{8,16},{16,24},{1,9},{9,17},{17,25},{2,10},{10,18},{18,26},{... | collective-permute-start | bytes 1572872 | tf_op jit(solution)/shard_map/ppermute | solution.py:13
  11.9 20.7 %collective-permute-start.1 = (f32[256,512]{1,0:T(8,128)}, f32[256,512]{1,0:T(8,128)}, u32[]{:S(2)}, u32[]{:S(2)}) collective-permute-start(f32[256,512]{1,0:T(8,128)} %bitcast.12), channel_id=1, source_target_pairs={{8,0},{16,8},{24,16},{9,1},{17,9},{25,17},{10,2},{18,10},{26,18},{... | collective-permute-start | bytes 1572872 | tf_op jit(solution)/shard_map/ppermute | solution.py:13
  14.8 18.9 %collective-permute-start.2 = (f32[256,512]{1,0:T(8,128)}, f32[256,512]{1,0:T(8,128)}, u32[]{:S(2)}, u32[]{:S(2)}) collective-permute-start(f32[256,512]{1,0:T(8,128)} %bitcast.13), channel_id=1, source_target_pairs={{7,0},{0,1},{1,2},{2,3},{3,4},{4,5},{5,6},{6,7},{15,8},{8,9},{9,10... | collective-permute-start | bytes 1572872 | tf_op jit(solution)/shard_map/ppermute | solution.py:19
  18.4 16.3 %collective-permute-start.3 = (f32[256,512]{1,0:T(8,128)}, f32[256,512]{1,0:T(8,128)}, u32[]{:S(2)}, u32[]{:S(2)}) collective-permute-start(f32[256,512]{1,0:T(8,128)} %bitcast.14), channel_id=1, source_target_pairs={{1,0},{2,1},{3,2},{4,3},{5,4},{6,5},{7,6},{0,7},{9,8},{10,9},{11,1... | collective-permute-start | bytes 1572872 | tf_op jit(solution)/shard_map/ppermute | solution.py:19
  161.3 20.8 %all-to-all-start = ((f32[8,64,256]{2,1,0:T(8,128)}), f32[8,64,256]{2,1,0:T(8,128)S(1)}, u32[]{:S(2)}, u32[]{:S(2)}) async-start(f32[8,64,256]{2,1,0:T(8,128)} %bitcast_dynamic-update-slice_fusion), calls=%async_computation | async-start | bytes 1048576 | tf_op jit(solution)/shard_map/all_to_all | solution.py:95
  182.1 5.6 %collective-permute-start.5 = (f32[2,2048]{1,0:T(2,128)S(1)}, f32[2,2048]{1,0:T(2,128)S(1)}, u32[]{:S(2)}, u32[]{:S(2)}) collective-permute-start(f32[2,2048]{1,0:T(2,128)S(1)} %bitcast.92), channel_id=1, source_target_pairs={{1,0},{2,1},{3,2},{4,3},{5,4},{6,5},{7,6},{9,8},{10,9},{11,10},{12... | collective-permute-start | bytes 49160 | tf_op jit(solution)/shard_map/ppermute | solution.py:30
  185.0 3.5 %collective-permute-start.4 = (f32[2,2048]{1,0:T(2,128)S(1)}, f32[2,2048]{1,0:T(2,128)S(1)}, u32[]{:S(2)}, u32[]{:S(2)}) collective-permute-start(f32[2,2048]{1,0:T(2,128)S(1)} %bitcast.91), channel_id=1, source_target_pairs={{0,1},{1,2},{2,3},{3,4},{4,5},{5,6},{6,7},{8,9},{9,10},{10,11},{11... | collective-permute-start | bytes 49160 | tf_op jit(solution)/shard_map/ppermute | solution.py:29
